TPU v7x, 128 devices: a whole 4x4x4 slice. The times are simulated.
128 devices in a mesh: wide: 16 (over z, x), narrow: 8 (over y, core).
Axes of the slice: x: 4, y: 4, z: 4, core: 2. Of those that a mesh axis runs over, the one named last changes fastest.
Arguments:
- inputs: bfloat16 [4, 256, 16384], P(None, 'wide', 'narrow'), may hold values from -600 to 600
- norm_gain: bfloat16 [16384], P('narrow'), may hold values from 0.099609375 to 1.8984375
- w_query: bfloat16 [16384, 8192], P('narrow', 'wide'), may hold values from -0.0234375 to 0.0234375
- w_keyval: bfloat16 [16384, 1024], P('narrow', 'wide'), may hold values from -0.0234375 to 0.0234375
- w_out: bfloat16 [8192, 16384], P('wide', 'narrow'), may hold values from -0.0625 to 0.0625
- key_cache: bfloat16 [256, 4096, 512], P(('wide', 'narrow')), may hold values from -1700 to 1700
- value_cache: bfloat16 [256, 4096, 512], P(('wide', 'narrow')), may hold values from -48 to 48
- lengths: int32 [256], P(('wide', 'narrow')), may hold values from 1024 to 4092, as said below
- positions: int32 [256], P(('wide', 'narrow')), may hold values from 1024 to 8187, as said below
Outputs:
- attended: bfloat16 [4, 256, 16384], P(None, 'wide', 'narrow')
- new_keys: bfloat16 [4, 256, 512], P(None, ('wide', 'narrow'))
- new_values: bfloat16 [4, 256, 512], P(None, ('wide', 'narrow'))
Inputs may be any that keep to these rules, and one draw needn't show every extreme that they name: A row's cache holds its first lengths slots. `positions`: a row's later new tokens follow its first one position by position.
All inputs are finite; a program needn't handle non-finite values.
Results may differ from a plain program's by a relative error of at most 0.007.
The roundings to bfloat16 on the way count: a program that leaves them out, or rounds other values in their place, can miss the bound.
Values may be sent and summed in bfloat16 or wider, within the bound.
A program may use at most 128 MiB of HBM per device.

v0:
```python
import jax
import jax.numpy as jnp
from jax import lax
from jax.sharding import PartitionSpec as P

D = 16384
HQ = 64
KVH = 4
HD = 128
STEPS = 4


def rotate(values, rotary_pos):
    half_dim = values.shape[-1] // 2
    inverse_freq = jnp.exp(
        -jnp.log(jnp.float32(500000.0))
        * jnp.arange(half_dim, dtype=jnp.float32)
        * 2.0
        / (2 * half_dim)
    )
    angles = rotary_pos.astype(jnp.float32)[..., None] * inverse_freq
    cosine = jnp.cos(angles)[..., None, :]
    sine = jnp.sin(angles)[..., None, :]
    first_half = values[..., :half_dim]
    second_half = values[..., half_dim:]
    return jnp.concatenate(
        [first_half * cosine - second_half * sine, second_half * cosine + first_half * sine],
        axis=-1,
    )


def local(inputs, norm_gain, w_query, w_keyval, w_out, key_cache, value_cache, lengths, positions):
    wide_count = lax.axis_size("wide")
    narrow_count = lax.axis_size("narrow")
    rows_dev = key_cache.shape[0]
    cache_len = key_cache.shape[1]
    q_local = w_query.shape[1]
    kv_local = w_keyval.shape[1]
    col_count = q_local + kv_local
    group_size = HQ // KVH
    factor = 1.0 / jnp.sqrt(jnp.float32(HD))
    step_outputs = []
    key_list = []
    value_list = []
    for step_index in range(STEPS):
        prepare_step_block = inputs[step_index : step_index + 1]
        project_count_steps = prepare_step_block.shape[0]
        row_values = prepare_step_block.astype(jnp.float32)
        partial_square = jnp.sum(row_values * row_values, axis=-1)
        total_square = lax.psum(partial_square, "narrow")
        inv_rms = lax.rsqrt(total_square / D + 1e-05)
        normed = (row_values * inv_rms[..., None] * norm_gain.astype(jnp.float32)).astype(
            jnp.bfloat16
        )
        shard_piece = lax.all_gather(normed, "wide", axis=1, tiled=True)
        first_part = jnp.einsum(
            "trd,dc->trc", shard_piece, w_query, preferred_element_type=jnp.float32
        )
        second_part = jnp.einsum(
            "trd,dc->trc", shard_piece, w_keyval, preferred_element_type=jnp.float32
        )
        project_partials = jnp.concatenate([first_part, second_part], axis=2)
        split_terms = project_partials.reshape(
            project_count_steps, wide_count, narrow_count, rows_dev, col_count
        )
        summed = lax.psum_scatter(split_terms, "narrow", scatter_dimension=2, tiled=True).astype(
            jnp.bfloat16
        )
        summed = summed.reshape(project_count_steps, wide_count, rows_dev, col_count)
        received = lax.all_to_all(summed, "wide", split_axis=1, concat_axis=3, tiled=True)
        arranged = received.reshape(project_count_steps, rows_dev, wide_count, col_count)
        query = arranged[..., :q_local].reshape(project_count_steps, rows_dev, HQ * HD)
        keyval = arranged[..., q_local:].reshape(project_count_steps, rows_dev, 2 * KVH * HD)
        prepare_count_steps = prepare_step_block.shape[0]
        rotary_pos = (
            positions[None, :]
            + step_index
            + jnp.arange(prepare_count_steps, dtype=jnp.int32)[:, None]
        )
        prepare_rot_query = rotate(
            query.astype(jnp.float32).reshape(prepare_count_steps, rows_dev, HQ, HD), rotary_pos
        )
        prepare_rot_query = prepare_rot_query.astype(jnp.bfloat16).reshape(
            prepare_count_steps, rows_dev, HQ * HD
        )
        rot_keys = rotate(
            keyval[..., : KVH * HD]
            .astype(jnp.float32)
            .reshape(prepare_count_steps, rows_dev, KVH, HD),
            rotary_pos,
        )
        rot_keys = rot_keys.astype(jnp.bfloat16).reshape(prepare_count_steps, rows_dev, KVH * HD)
        rot_query, rot_keys, new_vals = (prepare_rot_query, rot_keys, keyval[..., KVH * HD :])
        key_list.append(rot_keys)
        value_list.append(new_vals)
        fresh_keys = jnp.concatenate(key_list, axis=0)
        attend_count_steps = rot_query.shape[0]
        fresh_count = fresh_keys.shape[0]
        grouped = rot_query.reshape(attend_count_steps, rows_dev, KVH, group_size, HD)
        cached = key_cache.reshape(rows_dev, cache_len, KVH, HD)
        cache_scores = (
            jnp.einsum("trgqd,rsgd->rgtqs", grouped, cached, preferred_element_type=jnp.float32)
            * factor
        )
        visible = jnp.arange(cache_len, dtype=jnp.int32)[None, :] < lengths[:, None]
        cache_scores = jnp.where(visible[:, None, None, None, :], cache_scores, -jnp.inf)
        fresh_view = fresh_keys.reshape(fresh_count, rows_dev, KVH, HD)
        fresh_scores = (
            jnp.einsum("trgqd,jrgd->rgtqj", grouped, fresh_view, preferred_element_type=jnp.float32)
            * factor
        )
        causal_mask = (
            jnp.arange(fresh_count, dtype=jnp.int32)[None, :]
            <= (step_index + jnp.arange(attend_count_steps, dtype=jnp.int32))[:, None]
        )
        fresh_scores = jnp.where(causal_mask[None, None, :, None, :], fresh_scores, -jnp.inf)
        highest = jnp.maximum(jnp.max(cache_scores, -1), jnp.max(fresh_scores, -1))[..., None]
        cache_exp = jnp.exp(cache_scores - highest)
        fresh_exp = jnp.exp(fresh_scores - highest)
        normaliser = jnp.sum(cache_exp, -1, keepdims=True) + jnp.sum(fresh_exp, -1, keepdims=True)
        cache_weights = (cache_exp / normaliser).astype(jnp.bfloat16)
        fresh_weights = (fresh_exp / normaliser).astype(jnp.bfloat16)
        cached_values = value_cache.reshape(rows_dev, cache_len, KVH, HD)
        fresh_vals = jnp.concatenate(value_list, axis=0).reshape(fresh_count, rows_dev, KVH, HD)
        output = jnp.einsum(
            "rgtqs,rsgd->trgqd", cache_weights, cached_values, preferred_element_type=jnp.float32
        )
        output = output + jnp.einsum(
            "rgtqj,jrgd->trgqd", fresh_weights, fresh_vals, preferred_element_type=jnp.float32
        )
        attended_heads = output.astype(jnp.bfloat16).reshape(attend_count_steps, rows_dev, HQ * HD)
        count_steps = attended_heads.shape[0]
        by_heads = lax.all_to_all(
            attended_heads.reshape(count_steps, 1, rows_dev, HQ * HD),
            "wide",
            split_axis=3,
            concat_axis=1,
            tiled=True,
        )
        by_heads = by_heads.reshape(count_steps, wide_count, 1, rows_dev, by_heads.shape[-1])
        partials = jnp.einsum(
            "twprh,hc->twprc",
            lax.all_gather(by_heads, "narrow", axis=2, tiled=True),
            w_out,
            preferred_element_type=jnp.float32,
        )
        partials = partials.reshape(
            count_steps, wide_count * narrow_count * rows_dev, partials.shape[-1]
        )
        step_outputs.append(
            lax.psum_scatter(partials, "wide", scatter_dimension=1, tiled=True).astype(jnp.bfloat16)
        )
    return (
        jnp.concatenate(step_outputs, axis=0),
        jnp.concatenate(key_list, axis=0),
        jnp.concatenate(value_list, axis=0),
    )


def solution(mesh):
    return jax.shard_map(
        local,
        mesh=mesh,
        in_specs=(
            P(None, "wide", "narrow"),
            P("narrow"),
            P("narrow", "wide"),
            P("narrow", "wide"),
            P("wide", "narrow"),
            P(("wide", "narrow"), None, None),
            P(("wide", "narrow"), None, None),
            P(("wide", "narrow")),
            P(("wide", "narrow")),
        ),
        out_specs=(
            P(None, "wide", "narrow"),
            P(None, ("wide", "narrow"), None),
            P(None, ("wide", "narrow"), None),
        ),
        check_vma=False,
    )
```

profile of v0, /device:TPU:0, one launch (start us, length us, event | category | flops | bytes accessed | tf_op | source)
XLA Modules:
  0.0 833.2 jit_solution(438713747634489099)
XLA Ops:
  9.2 15.0 %all-reduce = (f32[1,16]{1,0:T(1,128)S(1)}, f32[1,16]{1,0:T(1,128)S(1)}, f32[1,16]{1,0:T(1,128)S(1)}, f32[1,16]{1,0:T(1,128)S(1)}) all-reduce(f32[1,16]{1,0:T(1,128)S(1)} %bitcast.378, f32[1,16]{1,0:T(1,128)S(1)} %bitcast.379, f32[1,16]{1,0:T(1,128)S(1)} %bitcast.377, ...), channel_id=1, replica_groups=mesh['wide'=16,'narrow'=8] {'narrow'}, use_global_device_ids=true, to_apply=%region_23.24 | all-reduce | flops 64 | bytes 512 | tf_op jit(solution)/shard_map/psum | solution.py:50
  28.1 40.4 %all-gather.7.cloned.1.call-done = bf16[1,256,2048]{2,1,0:T(8,128)(2,1)} async-done(((bf16[1,16,2048]{2,1,0:T(8,128)(2,1)}), bf16[1,256,2048]{2,1,0:T(8,128)(2,1)}) %all-gather.7.cloned.1.call-update) | async-done | bytes 1048592 | tf_op jit(solution)/shard_map/all_gather | solution.py:55
  74.2 38.9 %all-gather.5.cloned.1.call-done = bf16[1,256,2048]{2,1,0:T(8,128)(2,1)} async-done(((bf16[1,16,2048]{2,1,0:T(8,128)(2,1)}), bf16[1,256,2048]{2,1,0:T(8,128)(2,1)}) %all-gather.5.cloned.1.call-update) | async-done | bytes 1048592 | tf_op jit(solution)/shard_map/all_gather | solution.py:55
  119.0 38.2 %all-gather.11.cloned.1.call-done = bf16[1,256,2048]{2,1,0:T(8,128)(2,1)} async-done(((bf16[1,16,2048]{2,1,0:T(8,128)(2,1)}), bf16[1,256,2048]{2,1,0:T(8,128)(2,1)}) %all-gather.11.cloned.1.call-update) | async-done | bytes 1048592 | tf_op jit(solution)/shard_map/all_gather | solution.py:55
  163.0 38.1 %all-gather.9.cloned.1.call-done = bf16[1,256,2048]{2,1,0:T(8,128)(2,1)} async-done(((bf16[1,16,2048]{2,1,0:T(8,128)(2,1)}), bf16[1,256,2048]{2,1,0:T(8,128)(2,1)}) %all-gather.9.cloned.1.call-update) | async-done | bytes 1048592 | tf_op jit(solution)/shard_map/all_gather | solution.py:55
  206.7 27.4 %reduce-scatter.13.cloned.1.call-done = f32[1,16,1,2,576]{4,1,3,0,2:T(8,128)} async-done(((f32[1,16,8,2,576]{4,1,3,0,2:T(8,128)}), f32[1,16,1,2,576]{4,1,3,0,2:T(8,128)}) %reduce-scatter.13.cloned.1.call-update) | async-done | bytes 73744 | tf_op jit(solution)/shard_map/reduce_scatter | solution.py:66
  235.7 6.9 all-to-all-start.2
  242.6 24.2 %reduce-scatter.9.cloned.1.call-done = f32[1,16,1,2,576]{4,1,3,0,2:T(8,128)} async-done(((f32[1,16,8,2,576]{4,1,3,0,2:T(8,128)}), f32[1,16,1,2,576]{4,1,3,0,2:T(8,128)}) %reduce-scatter.9.cloned.1.call-update) | async-done | bytes 73744 | tf_op jit(solution)/shard_map/reduce_scatter | solution.py:66
  268.3 7.1 all-to-all-start
  275.7 7.2 all-to-all-done
  283.4 5.8 fusion.189
  289.9 4.8 fusion.75
  295.0 6.8 copy.243
  302.3 46.5 %reduce.42 = bf16[8192,2]{1,0:T(8,128)(2,1)} reduce(bf16[8192,1,1,2]{3,2,1,0:T(2,128)(2,1)} %bitcast.332, bf16[]{:T(256)} %broadcast.355), dimensions={1,2}, to_apply=%bitcast.274.reduce_sub_computation | reduce | bytes 65538
  348.9 4.8 reshape.1213
  358.7 6.0 all-to-all-done.3
  368.2 8.4 %reshape.1214 = bf16[8192,1,1,2]{3,2,1,0:T(2,128)(2,1)} reshape(bf16[16,2,512]{2,1,0:T(2,128)(2,1)S(1)} %all-to-all-done.3) | data formatting | bytes 65536
  376.6 8.1 copy.244
  384.7 12.8 %all_gather.27 = bf16[1,16,8,2,512]{4,1,3,0,2:T(8,128)(2,1)S(1)} all-gather(bf16[1,16,1,2,512]{4,1,3,0,2:T(8,128)(2,1)S(1)} %bitcast.368), channel_id=1, replica_groups=mesh['wide'=16,'narrow'=8] {'narrow'}, dimensions={2}, use_global_device_ids=true | all-gather | bytes 294912 | tf_op jit(solution)/shard_map/all_gather | solution.py:143
  401.6 7.2 all-to-all-start.4
  409.4 6.9 all-to-all-done.4
  417.3 5.8 fusion.185
  423.6 4.8 fusion.81
  428.7 6.8 copy.269
  435.4 46.6 %reduce.40 = bf16[8192,2]{1,0:T(8,128)(2,1)} reduce(bf16[8192,1,1,2]{3,2,1,0:T(2,128)(2,1)} %bitcast.335, bf16[]{:T(256)} %broadcast.355), dimensions={1,2}, to_apply=%bitcast.270.reduce_sub_computation | reduce | bytes 65538
  482.0 4.2 reshape.1209
  486.2 10.7 %all_to_all.120 = bf16[16,2,512]{2,1,0:T(2,128)(2,1)S(1)} all-to-all(bf16[16,2,512]{2,1,0:T(2,128)(2,1)S(1)} %reshape.1209), channel_id=1, replica_groups=mesh['wide'=16,'narrow'=8] {'wide'}, dimensions={0} | all-to-all | bytes 65536 | tf_op jit(solution)/shard_map/all_to_all | solution.py:133
  496.9 8.4 %reshape.1210 = bf16[8192,1,1,2]{3,2,1,0:T(2,128)(2,1)} reshape(bf16[16,2,512]{2,1,0:T(2,128)(2,1)S(1)} %all_to_all.120) | data formatting | bytes 65536
  505.3 8.1 copy.270
  513.4 13.0 %all_gather.31 = bf16[1,16,8,2,512]{4,1,3,0,2:T(8,128)(2,1)S(1)} all-gather(bf16[1,16,1,2,512]{4,1,3,0,2:T(8,128)(2,1)S(1)} %bitcast.369), channel_id=1, replica_groups=mesh['wide'=16,'narrow'=8] {'narrow'}, dimensions={2}, use_global_device_ids=true | all-gather | bytes 294912 | tf_op jit(solution)/shard_map/all_gather | solution.py:143
  529.4 5.8 fusion.187
  535.6 4.8 fusion.78
  540.7 6.8 copy.256
  547.5 46.6 %reduce.41 = bf16[8192,2]{1,0:T(8,128)(2,1)} reduce(bf16[8192,1,1,2]{3,2,1,0:T(2,128)(2,1)} %bitcast.337, bf16[]{:T(256)} %broadcast.355), dimensions={1,2}, to_apply=%bitcast.272.reduce_sub_computation | reduce | bytes 65538
  598.3 10.8 %all_to_all.121 = bf16[16,2,512]{2,1,0:T(2,128)(2,1)S(1)} all-to-all(bf16[16,2,512]{2,1,0:T(2,128)(2,1)S(1)} %reshape.1211), channel_id=1, replica_groups=mesh['wide'=16,'narrow'=8] {'wide'}, dimensions={0} | all-to-all | bytes 65536 | tf_op jit(solution)/shard_map/all_to_all | solution.py:133
  609.1 8.4 %reshape.1212 = bf16[8192,1,1,2]{3,2,1,0:T(2,128)(2,1)} reshape(bf16[16,2,512]{2,1,0:T(2,128)(2,1)S(1)} %all_to_all.121) | data formatting | bytes 65536
  617.5 8.1 copy.257
  625.6 13.1 %all_gather.29 = bf16[1,16,8,2,512]{4,1,3,0,2:T(8,128)(2,1)S(1)} all-gather(bf16[1,16,1,2,512]{4,1,3,0,2:T(8,128)(2,1)S(1)} %bitcast.370), channel_id=1, replica_groups=mesh['wide'=16,'narrow'=8] {'narrow'}, dimensions={2}, use_global_device_ids=true | all-gather | bytes 294912 | tf_op jit(solution)/shard_map/all_gather | solution.py:143
  641.6 5.8 fusion.191
  647.9 4.8 fusion.96
  652.8 6.8 copy.230
  659.6 46.5 %reduce.43 = bf16[8192,2]{1,0:T(8,128)(2,1)} reduce(bf16[8192,1,1,2]{3,2,1,0:T(2,128)(2,1)} %bitcast.333, bf16[]{:T(256)} %broadcast.355), dimensions={1,2}, to_apply=%bitcast.276.reduce_sub_computation | reduce | bytes 65538
  706.1 4.2 reshape.1215
  710.2 10.8 %all_to_all.122 = bf16[16,2,512]{2,1,0:T(2,128)(2,1)S(1)} all-to-all(bf16[16,2,512]{2,1,0:T(2,128)(2,1)S(1)} %reshape.1215), channel_id=1, replica_groups=mesh['wide'=16,'narrow'=8] {'wide'}, dimensions={0} | all-to-all | bytes 65536 | tf_op jit(solution)/shard_map/all_to_all | solution.py:133
  721.0 8.4 %reshape.1216 = bf16[8192,1,1,2]{3,2,1,0:T(2,128)(2,1)} reshape(bf16[16,2,512]{2,1,0:T(2,128)(2,1)S(1)} %all_to_all.122) | data formatting | bytes 65536
  729.4 8.1 copy.231
  737.5 12.8 %all_gather.25 = bf16[1,16,8,2,512]{4,1,3,0,2:T(8,128)(2,1)S(1)} all-gather(bf16[1,16,1,2,512]{4,1,3,0,2:T(8,128)(2,1)S(1)} %bitcast.371), channel_id=1, replica_groups=mesh['wide'=16,'narrow'=8] {'narrow'}, dimensions={2}, use_global_device_ids=true | all-gather | bytes 294912 | tf_op jit(solution)/shard_map/all_gather | solution.py:143
  756.3 68.0 %reduce-scatter.11.cloned.1.call-done = f32[1,16,2048]{2,1,0:T(8,128)} async-done(((f32[1,256,2048]{2,1,0:T(8,128)}), f32[1,16,2048]{2,1,0:T(8,128)}) %reduce-scatter.11.cloned.1.call-update) | async-done | bytes 131088 | tf_op jit(solution)/shard_map/reduce_scatter | solution.py:151
  (187 shorter events, 67.5 us)
Async XLA Ops:
  7.2 390.8 %copy-start = (bf16[512,2048]{1,0:T(8,128)(2,1)S(1)}, bf16[512,2048]{1,0:T(8,128)(2,1)}, u32[]{:S(2)}) copy-start(bf16[512,2048]{1,0:T(8,128)(2,1)} %param.13) | copy-start | bytes 6291460
  7.2 63.1 %copy-start.4 = (bf16[2048,64]{0,1:T(8,128)(2,1)S(1)}, bf16[2048,64]{0,1:T(8,128)(2,1)}, u32[]{:S(2)}) copy-start(bf16[2048,64]{0,1:T(8,128)(2,1)} %param.12) | copy-start | bytes 786436
  7.2 61.3 %all-gather.7.cloned.1.call-start = ((), (), s32[]{:S(2)}) async-start(), calls=%async_computation.19 | async-start | bytes 1114112 | tf_op jit(solution)/shard_map/all_gather | solution.py:55
  26.0 87.1 %all-gather.5.cloned.1.call-start = ((), (), s32[]{:S(2)}) async-start(), calls=%async_computation.16 | async-start | bytes 1114112 | tf_op jit(solution)/shard_map/all_gather | solution.py:55
  26.7 130.5 %all-gather.11.cloned.1.call-start = ((), (), s32[]{:S(2)}) async-start(), calls=%async_computation.25 | async-start | bytes 1114112 | tf_op jit(solution)/shard_map/all_gather | solution.py:55
  27.4 173.6 %all-gather.9.cloned.1.call-start = ((), (), s32[]{:S(2)}) async-start(), calls=%async_computation.22 | async-start | bytes 1114112 | tf_op jit(solution)/shard_map/all_gather | solution.py:55
  28.0 206.1 %reduce-scatter.13.cloned.1.call-start = ((), (), s32[]{:S(2)}) async-start(), calls=%async_computation.20 | async-start | bytes 737280 | tf_op jit(solution)/shard_map/reduce_scatter | solution.py:66
  74.1 192.6 %reduce-scatter.9.cloned.1.call-start = ((), (), s32[]{:S(2)}) async-start(), calls=%async_computation.17 | async-start | bytes 737280 | tf_op jit(solution)/shard_map/reduce_scatter | solution.py:66
  117.6 1.2 copy-start.2
  118.8 238.4 %reduce-scatter.21.cloned.1.call-start = ((), (), s32[]{:S(2)}) async-start(), calls=%async_computation.26 | async-start | bytes 737280 | tf_op jit(solution)/shard_map/reduce_scatter | solution.py:66
  161.7 1.2 copy-start.3
  162.8 237.2 %reduce-scatter.17.cloned.1.call-start = ((), (), s32[]{:S(2)}) async-start(), calls=%async_computation.23 | async-start | bytes 737280 | tf_op jit(solution)/shard_map/reduce_scatter | solution.py:66
  235.7 32.6 %all-to-all-start.2 = ((bf16[1,16,2,576]{3,2,0,1:T(2,128)(2,1)}), bf16[1,16,2,576]{3,2,0,1:T(2,128)(2,1)S(1)}, u32[]{:S(2)}, u32[]{:S(2)}) async-start(bf16[1,16,2,576]{3,2,0,1:T(2,128)(2,1)} %copy.238), calls=%async_computation.5 | async-start | bytes 81920 | tf_op jit(solution)/shard_map/all_to_all | solution.py:70
  268.3 14.7 %all-to-all-start = ((bf16[1,16,2,576]{3,2,0,1:T(2,128)(2,1)}), bf16[1,16,2,576]{3,2,0,1:T(2,128)(2,1)S(1)}, u32[]{:S(2)}, u32[]{:S(2)}) async-start(bf16[1,16,2,576]{3,2,0,1:T(2,128)(2,1)} %copy.226), calls=%async_computation.1 | async-start | bytes 81920 | tf_op jit(solution)/shard_map/all_to_all | solution.py:70
  353.6 11.0 %all-to-all-start.3 = ((bf16[16,2,512]{2,1,0:T(2,128)(2,1)}), bf16[16,2,512]{2,1,0:T(2,128)(2,1)S(1)}, u32[]{:S(2)}, u32[]{:S(2)}) async-start(bf16[16,2,512]{2,1,0:T(2,128)(2,1)} %reshape.1213), calls=%async_computation.6 | async-start | bytes 65536 | tf_op jit(solution)/shard_map/all_to_all | solution.py:133
  364.7 36.9 %all-to-all-start.6 = ((bf16[1,16,2,576]{3,2,0,1:T(2,128)(2,1)}), bf16[1,16,2,576]{3,2,0,1:T(2,128)(2,1)S(1)}, u32[]{:S(2)}, u32[]{:S(2)}) async-start(bf16[1,16,2,576]{3,2,0,1:T(2,128)(2,1)} %copy.264), calls=%async_computation.13 | async-start | bytes 81920 | tf_op jit(solution)/shard_map/all_to_all | solution.py:70
  368.2 385.3 %reduce-scatter.15.cloned.1.call-start = ((), (), s32[]{:S(2)}) async-start(), calls=%async_computation.21 | async-start | bytes 2228224 | tf_op jit(solution)/shard_map/reduce_scatter | solution.py:151
  401.6 14.8 %all-to-all-start.4 = ((bf16[1,16,2,576]{3,2,0,1:T(2,128)(2,1)}), bf16[1,16,2,576]{3,2,0,1:T(2,128)(2,1)S(1)}, u32[]{:S(2)}, u32[]{:S(2)}) async-start(bf16[1,16,2,576]{3,2,0,1:T(2,128)(2,1)} %copy.251), calls=%async_computation.9 | async-start | bytes 81920 | tf_op jit(solution)/shard_map/all_to_all | solution.py:70
  408.8 345.7 %reduce-scatter.23.cloned.1.call-start = ((), (), s32[]{:S(2)}) async-start(), calls=%async_computation.27 | async-start | bytes 2228224 | tf_op jit(solution)/shard_map/reduce_scatter | solution.py:151
  416.5 6.6 copy-start.1
  528.9 226.5 %reduce-scatter.19.cloned.1.call-start = ((), (), s32[]{:S(2)}) async-start(), calls=%async_computation.24 | async-start | bytes 2228224 | tf_op jit(solution)/shard_map/reduce_scatter | solution.py:151
  641.1 183.2 %reduce-scatter.11.cloned.1.call-start = ((), (), s32[]{:S(2)}) async-start(), calls=%async_computation.18 | async-start | bytes 2228224 | tf_op jit(solution)/shard_map/reduce_scatter | solution.py:151
Sparse Core Ops, SparseCore 0:
  26.1 42.3 all-gather.6
  71.2 41.8 all-gather.4
  115.3 41.8 all-gather.10
  159.2 41.8 all-gather.8
  203.3 30.8 reduce-scatter.12
  236.4 30.2 reduce-scatter.8
  269.1 30.2 reduce-scatter.20
  301.8 30.5 reduce-scatter.16
  400.2 75.4 reduce-scatter.14
  529.0 71.2 reduce-scatter.22
  641.2 71.4 reduce-scatter.18
  752.9 71.2 reduce-scatter.10
where the time goes:
time: 842 us; the launch traced here: 833 us
  waiting for transfers between devices  297 us (35%)
  other arithmetic  202 us (24%)
  local copies, waits for them, and re-layouts  127 us (15%)
  blocking collectives  99 us (12%)
  matrix products  63.4 us (8%)
  starting transfers between devices  29 us (3%)
  between operations  15.4 us (2%)
    unnamed x4, other arithmetic  186 us
    all_gather x4, waiting for transfers between devices, local(): shard_piece = lax.all_gather(normed, 'wide', axis=1, tiled=True)  156 us
    reduce_scatter x4, waiting for transfers between devices, local(): lax.psum_scatter(partials, 'wide', scatter_dimension=1, tiled=True)  68 us
    all_gather x4, blocking collectives, local(): lax.all_gather(by_heads, 'narrow', axis=2, tiled=True)  51.7 us
    reduce_scatter x4, waiting for transfers between devices, local(): lax.psum_scatter(split_terms, 'narrow', scatter_dimension=2, tiled=True)  51.6 us
    unnamed x25, local copies, waits for them, and re-layouts  51.4 us
    all_to_all x3, blocking collectives, local(): lax.all_to_all(attended_heads.reshape(count_steps, 1, rows_dev, HQ * HD),...  32.3 us
    all_to_all x4, local copies, waits for them, and re-layouts, local(): lax.all_to_all(attended_heads.reshape(count_steps, 1, rows_dev, HQ * HD),...  32.3 us
  transfers between devices with their start and end apart: 17, of which 10 were waited for; matrix products, arithmetic and copies ran while one was open for 46% of the time, Pallas kernels for 0%

commit v1 on v0

--- a/solution.py
+++ b/solution.py
@@ -52,7 +52,9 @@
         normed = (row_values * inv_rms[..., None] * norm_gain.astype(jnp.float32)).astype(
             jnp.bfloat16
         )
-        shard_piece = lax.all_gather(normed, "wide", axis=1, tiled=True)
+        shard_piece = jnp.concatenate(
+            lax.all_to_all(jnp.stack([normed] * lax.axis_size("wide")), "wide", 0, 0), axis=1
+        )
         first_part = jnp.einsum(
             "trd,dc->trc", shard_piece, w_query, preferred_element_type=jnp.float32
         )

time: 842 us -> 710 us (0.84)
  waiting for transfers between devices: 297 us -> 126 us
  blocking collectives: 99 us -> 142 us
    all_gather x4 -> x0, waiting for transfers between devices: 156 us -> none  [local(): shard_piece = lax.all_gather(normed, 'wide', axis=1, tiled=True)]
    reduce_scatter x4, waiting for transfers between devices: 51.6 us -> 0.08 us  [local(): lax.psum_scatter(split_terms, 'narrow', scatter_dimension=2, tiled=True)]
    all_to_all x0 -> x1, blocking collectives: none -> 22.8 us  [local(): lax.all_to_all(jnp.stack([normed] * lax.axis_size('wide')), 'wide', 0, 0)]
    all_to_all x1 -> x3, waiting for transfers between devices: 5.97 us -> 28.5 us  [local(): lax.all_to_all(jnp.stack([normed] * lax.axis_size('wide')), 'wide', 0, 0)]
    all_to_all x4, waiting for transfers between devices: 14.2 us -> 27.8 us  [local(): lax.all_to_all(summed, 'wide', split_axis=1, concat_axis=3, tiled=True)]
    all_to_all x3 -> x4, blocking collectives: 32.3 us -> 43.6 us  [local(): lax.all_to_all(attended_heads.reshape(count_steps, 1, rows_dev, HQ * HD),...]
    all_to_all x4, starting transfers between devices: 24.6 us -> 14 us  [local(): lax.all_to_all(summed, 'wide', split_axis=1, concat_axis=3, tiled=True)]
    all_gather x4, blocking collectives: 51.7 us -> 61 us  [local(): lax.all_gather(by_heads, 'narrow', axis=2, tiled=True)]
  transfers between devices with their start and end apart: 17 -> 15, of which waited for: 10 -> 8; matrix products, arithmetic and copies ran while one was open for 46% -> 55% of each run, Pallas kernels for 0% -> 0%
where the time goes in v1:
time: 710 us; the launch traced here: 700 us
  other arithmetic  202 us (28%)
  blocking collectives  142 us (20%)
  local copies, waits for them, and re-layouts  130 us (18%)
  waiting for transfers between devices  126 us (18%)
  matrix products  57.4 us (8%)
  starting transfers between devices  27.1 us (4%)
  between operations  15.4 us (2%)
    unnamed x4, other arithmetic  186 us
    reduce_scatter x4, waiting for transfers between devices, local(): lax.psum_scatter(partials, 'wide', scatter_dimension=1, tiled=True)  69.8 us
    all_gather x4, blocking collectives, local(): lax.all_gather(by_heads, 'narrow', axis=2, tiled=True)  61 us
    unnamed x35, local copies, waits for them, and re-layouts  51.5 us
    all_to_all x4, blocking collectives, local(): lax.all_to_all(attended_heads.reshape(count_steps, 1, rows_dev, HQ * HD),...  43.6 us
    all_to_all x4, local copies, waits for them, and re-layouts, local(): lax.all_to_all(attended_heads.reshape(count_steps, 1, rows_dev, HQ * HD),...  32.3 us
    all_to_all x3, waiting for transfers between devices, local(): lax.all_to_all(jnp.stack([normed] * lax.axis_size('wide')), 'wide', 0, 0)  28.5 us
    all_to_all x4, waiting for transfers between devices, local(): lax.all_to_all(summed, 'wide', split_axis=1, concat_axis=3, tiled=True)  27.8 us
  transfers between devices with their start and end apart: 15, of which 8 were waited for; matrix products, arithmetic and copies ran while one was open for 55% of the time, Pallas kernels for 0%

profile of v1, /device:TPU:0, one launch (start us, length us, event | category | flops | bytes accessed | tf_op | source)
XLA Modules:
  0.0 700.3 jit_solution(12119445296841284807)
XLA Ops:
  9.2 15.0 %all-reduce = (f32[1,16]{1,0:T(1,128)S(1)}, f32[1,16]{1,0:T(1,128)S(1)}, f32[1,16]{1,0:T(1,128)S(1)}, f32[1,16]{1,0:T(1,128)S(1)}) all-reduce(f32[1,16]{1,0:T(1,128)S(1)} %bitcast.410, f32[1,16]{1,0:T(1,128)S(1)} %bitcast.411, f32[1,16]{1,0:T(1,128)S(1)} %bitcast.409, ...), channel_id=1, replica_groups=mesh['wide'=16,'narrow'=8] {'narrow'}, use_global_device_ids=true, to_apply=%region_23.24 | all-reduce | flops 64 | bytes 512 | tf_op jit(solution)/shard_map/psum | solution.py:50
  25.3 22.8 %all_to_all.140 = bf16[16,1,16,2048]{3,2,1,0:T(8,128)(2,1)} all-to-all(bf16[16,1,16,2048]{3,2,1,0:T(8,128)(2,1)S(1)} %stack.8), channel_id=1, replica_groups=mesh['wide'=16,'narrow'=8] {'wide'}, dimensions={0} | all-to-all | bytes 2097152 | tf_op jit(solution)/shard_map/all_to_all | solution.py:56
  49.2 3.8 all-to-all-start.3
  57.5 9.8 %all-to-all-done.3 = bf16[16,1,16,2048]{3,2,1,0:T(8,128)(2,1)S(1)} async-done(((bf16[16,1,16,2048]{3,2,1,0:T(8,128)(2,1)}), bf16[16,1,16,2048]{3,2,1,0:T(8,128)(2,1)S(1)}, u32[]{:S(2)}, u32[]{:S(2)}) %all-to-all-start.3) | async-done | bytes 1048608 | tf_op jit(solution)/shard_map/all_to_all | solution.py:56
  77.0 9.1 %all-to-all-done.6 = bf16[16,1,16,2048]{3,2,1,0:T(8,128)(2,1)S(1)} async-done(((bf16[16,1,16,2048]{3,2,1,0:T(8,128)(2,1)}), bf16[16,1,16,2048]{3,2,1,0:T(8,128)(2,1)S(1)}, u32[]{:S(2)}, u32[]{:S(2)}) %all-to-all-start.6) | async-done | bytes 1048608 | tf_op jit(solution)/shard_map/all_to_all | solution.py:56
  87.3 4.3 all-to-all-start.9
  95.4 9.6 %all-to-all-done.9 = bf16[16,1,16,2048]{3,2,1,0:T(8,128)(2,1)} async-done(((bf16[16,1,16,2048]{3,2,1,0:T(8,128)(2,1)}), bf16[16,1,16,2048]{3,2,1,0:T(8,128)(2,1)}, u32[]{:S(2)}, u32[]{:S(2)}) %all-to-all-start.9) | async-done | bytes 1048608 | tf_op jit(solution)/shard_map/all_to_all | solution.py:56
  114.8 6.1 all-to-all-done.1
  121.5 5.8 fusion.195
  127.9 4.8 fusion.96
  132.7 6.8 copy.243
  140.0 46.5 %reduce.43 = bf16[8192,2]{1,0:T(8,128)(2,1)} reduce(bf16[8192,1,1,2]{3,2,1,0:T(2,128)(2,1)} %bitcast.352, bf16[]{:T(256)} %broadcast.367), dimensions={1,2}, to_apply=%bitcast.288.reduce_sub_computation | reduce | bytes 65538
  186.6 4.2 reshape.1239
  190.8 10.7 %all_to_all.141 = bf16[16,2,512]{2,1,0:T(2,128)(2,1)S(1)} all-to-all(bf16[16,2,512]{2,1,0:T(2,128)(2,1)S(1)} %reshape.1239), channel_id=1, replica_groups=mesh['wide'=16,'narrow'=8] {'wide'}, dimensions={0} | all-to-all | bytes 65536 | tf_op jit(solution)/shard_map/all_to_all | solution.py:135
  201.5 8.4 %reshape.1240 = bf16[8192,1,1,2]{3,2,1,0:T(2,128)(2,1)} reshape(bf16[16,2,512]{2,1,0:T(2,128)(2,1)S(1)} %all_to_all.141) | data formatting | bytes 65536
  209.9 8.1 %copy.244 = bf16[1,1,2,8192]{3,2,1,0:T(2,128)(2,1)S(1)} copy(bf16[1,1,2,8192]{2,1,0,3:T(2,128)(2,1)} %bitcast.354) | data formatting | bytes 65536 | tf_op jit(solution)/shard_map/all_to_all | solution.py:135
  218.0 22.5 %all_gather.12 = bf16[1,16,8,2,512]{4,1,3,0,2:T(8,128)(2,1)S(1)} all-gather(bf16[1,16,1,2,512]{4,1,3,0,2:T(8,128)(2,1)S(1)} %bitcast.400), channel_id=1, replica_groups=mesh['wide'=16,'narrow'=8] {'narrow'}, dimensions={2}, use_global_device_ids=true | all-gather | bytes 294912 | tf_op jit(solution)/shard_map/all_gather | solution.py:145
  248.5 7.1 %all-to-all-done.4 = bf16[1,16,2,576]{3,2,0,1:T(2,128)(2,1)S(1)} async-done(((bf16[1,16,2,576]{3,2,0,1:T(2,128)(2,1)}), bf16[1,16,2,576]{3,2,0,1:T(2,128)(2,1)S(1)}, u32[]{:S(2)}, u32[]{:S(2)}) %all-to-all-start.4) | async-done | bytes 36896 | tf_op jit(solution)/shard_map/all_to_all | solution.py:72
  256.3 5.8 fusion.193
  262.6 4.9 fusion.75
  267.8 6.8 copy.257
  274.6 46.6 %reduce.42 = bf16[8192,2]{1,0:T(8,128)(2,1)} reduce(bf16[8192,1,1,2]{3,2,1,0:T(2,128)(2,1)} %bitcast.355, bf16[]{:T(256)} %broadcast.367), dimensions={1,2}, to_apply=%bitcast.286.reduce_sub_computation | reduce | bytes 65538
  321.1 4.2 reshape.1237
  325.3 11.0 %all_to_all.142 = bf16[16,2,512]{2,1,0:T(2,128)(2,1)S(1)} all-to-all(bf16[16,2,512]{2,1,0:T(2,128)(2,1)S(1)} %reshape.1237), channel_id=1, replica_groups=mesh['wide'=16,'narrow'=8] {'wide'}, dimensions={0} | all-to-all | bytes 65536 | tf_op jit(solution)/shard_map/all_to_all | solution.py:135
  336.3 8.4 %reshape.1238 = bf16[8192,1,1,2]{3,2,1,0:T(2,128)(2,1)} reshape(bf16[16,2,512]{2,1,0:T(2,128)(2,1)S(1)} %all_to_all.142) | data formatting | bytes 65536
  344.7 8.1 %copy.258 = bf16[1,1,2,8192]{3,2,1,0:T(2,128)(2,1)S(1)} copy(bf16[1,1,2,8192]{2,1,0,3:T(2,128)(2,1)} %bitcast.356) | data formatting | bytes 65536 | tf_op jit(solution)/shard_map/all_to_all | solution.py:135
  352.8 12.8 %all_gather.13 = bf16[1,16,8,2,512]{4,1,3,0,2:T(8,128)(2,1)S(1)} all-gather(bf16[1,16,1,2,512]{4,1,3,0,2:T(8,128)(2,1)S(1)} %bitcast.401), channel_id=1, replica_groups=mesh['wide'=16,'narrow'=8] {'narrow'}, dimensions={2}, use_global_device_ids=true | all-gather | bytes 294912 | tf_op jit(solution)/shard_map/all_gather | solution.py:145
  373.4 7.3 %all-to-all-done.7 = bf16[1,16,2,576]{3,2,0,1:T(2,128)(2,1)S(1)} async-done(((bf16[1,16,2,576]{3,2,0,1:T(2,128)(2,1)}), bf16[1,16,2,576]{3,2,0,1:T(2,128)(2,1)S(1)}, u32[]{:S(2)}, u32[]{:S(2)}) %all-to-all-start.7) | async-done | bytes 36896 | tf_op jit(solution)/shard_map/all_to_all | solution.py:72
  381.4 5.8 fusion.191
  387.7 4.9 fusion.78
  392.8 6.8 copy.271
  399.6 46.6 %reduce.41 = bf16[8192,2]{1,0:T(8,128)(2,1)} reduce(bf16[8192,1,1,2]{3,2,1,0:T(2,128)(2,1)} %bitcast.357, bf16[]{:T(256)} %broadcast.367), dimensions={1,2}, to_apply=%bitcast.284.reduce_sub_computation | reduce | bytes 65538
  446.2 4.2 reshape.1235
  450.4 11.0 %all_to_all.143 = bf16[16,2,512]{2,1,0:T(2,128)(2,1)S(1)} all-to-all(bf16[16,2,512]{2,1,0:T(2,128)(2,1)S(1)} %reshape.1235), channel_id=1, replica_groups=mesh['wide'=16,'narrow'=8] {'wide'}, dimensions={0} | all-to-all | bytes 65536 | tf_op jit(solution)/shard_map/all_to_all | solution.py:135
  461.4 8.4 %reshape.1236 = bf16[8192,1,1,2]{3,2,1,0:T(2,128)(2,1)} reshape(bf16[16,2,512]{2,1,0:T(2,128)(2,1)S(1)} %all_to_all.143) | data formatting | bytes 65536
  469.8 8.1 %copy.272 = bf16[1,1,2,8192]{3,2,1,0:T(2,128)(2,1)S(1)} copy(bf16[1,1,2,8192]{2,1,0,3:T(2,128)(2,1)} %bitcast.358) | data formatting | bytes 65536 | tf_op jit(solution)/shard_map/all_to_all | solution.py:135
  477.9 12.8 %all_gather.14 = bf16[1,16,8,2,512]{4,1,3,0,2:T(8,128)(2,1)S(1)} all-gather(bf16[1,16,1,2,512]{4,1,3,0,2:T(8,128)(2,1)S(1)} %bitcast.402), channel_id=1, replica_groups=mesh['wide'=16,'narrow'=8] {'narrow'}, dimensions={2}, use_global_device_ids=true | all-gather | bytes 294912 | tf_op jit(solution)/shard_map/all_gather | solution.py:145
  498.6 7.3 %all-to-all-done.10 = bf16[1,16,2,576]{3,2,0,1:T(2,128)(2,1)S(1)} async-done(((bf16[1,16,2,576]{3,2,0,1:T(2,128)(2,1)}), bf16[1,16,2,576]{3,2,0,1:T(2,128)(2,1)S(1)}, u32[]{:S(2)}, u32[]{:S(2)}) %all-to-all-start.10) | async-done | bytes 36896 | tf_op jit(solution)/shard_map/all_to_all | solution.py:72
  506.6 5.8 fusion.189
  512.9 4.9 fusion.81
  518.0 6.8 copy.285
  524.8 46.5 %reduce.40 = bf16[8192,2]{1,0:T(8,128)(2,1)} reduce(bf16[8192,1,1,2]{3,2,1,0:T(2,128)(2,1)} %bitcast.353, bf16[]{:T(256)} %broadcast.367), dimensions={1,2}, to_apply=%bitcast.282.reduce_sub_computation | reduce | bytes 65538
  571.3 4.2 reshape.1233
  575.5 10.9 %all_to_all.144 = bf16[16,2,512]{2,1,0:T(2,128)(2,1)S(1)} all-to-all(bf16[16,2,512]{2,1,0:T(2,128)(2,1)S(1)} %reshape.1233), channel_id=1, replica_groups=mesh['wide'=16,'narrow'=8] {'wide'}, dimensions={0} | all-to-all | bytes 65536 | tf_op jit(solution)/shard_map/all_to_all | solution.py:135
  586.5 8.4 %reshape.1234 = bf16[8192,1,1,2]{3,2,1,0:T(2,128)(2,1)} reshape(bf16[16,2,512]{2,1,0:T(2,128)(2,1)S(1)} %all_to_all.144) | data formatting | bytes 65536
  594.8 8.1 %copy.286 = bf16[1,1,2,8192]{3,2,1,0:T(2,128)(2,1)S(1)} copy(bf16[1,1,2,8192]{2,1,0,3:T(2,128)(2,1)} %bitcast.359) | data formatting | bytes 65536 | tf_op jit(solution)/shard_map/all_to_all | solution.py:135
  602.9 12.8 %all_gather.15 = bf16[1,16,8,2,512]{4,1,3,0,2:T(8,128)(2,1)S(1)} all-gather(bf16[1,16,1,2,512]{4,1,3,0,2:T(8,128)(2,1)S(1)} %bitcast.403), channel_id=1, replica_groups=mesh['wide'=16,'narrow'=8] {'narrow'}, dimensions={2}, use_global_device_ids=true | all-gather | bytes 294912 | tf_op jit(solution)/shard_map/all_gather | solution.py:145
  621.7 69.7 %reduce-scatter.23.cloned.1.call-done = f32[1,16,2048]{2,1,0:T(8,128)} async-done(((f32[1,256,2048]{2,1,0:T(8,128)}), f32[1,16,2048]{2,1,0:T(8,128)}) %reduce-scatter.23.cloned.1.call-update) | async-done | bytes 131088 | tf_op jit(solution)/shard_map/reduce_scatter | solution.py:153
  (199 shorter events, 69.8 us)
Async XLA Ops:
  7.2 233.7 %copy-start = (bf16[512,2048]{1,0:T(8,128)(2,1)S(1)}, bf16[512,2048]{1,0:T(8,128)(2,1)}, u32[]{:S(2)}) copy-start(bf16[512,2048]{1,0:T(8,128)(2,1)} %param.13) | copy-start | bytes 6291460
  49.2 5.8 copy-start.2
  49.2 18.1 %all-to-all-start.3 = ((bf16[16,1,16,2048]{3,2,1,0:T(8,128)(2,1)}), bf16[16,1,16,2048]{3,2,1,0:T(8,128)(2,1)S(1)}, u32[]{:S(2)}, u32[]{:S(2)}) async-start(bf16[16,1,16,2048]{3,2,1,0:T(8,128)(2,1)} %stack.9), calls=%async_computation.5 | async-start | bytes 2097152 | tf_op jit(solution)/shard_map/all_to_all | solution.py:56
  53.0 55.3 %reduce-scatter.9.cloned.1.call-start = ((), (), s32[]{:S(2)}) async-start(), calls=%async_computation.20 | async-start | bytes 737280 | tf_op jit(solution)/shard_map/reduce_scatter | solution.py:68
  53.1 2.5 copy-start.6
  67.3 1.4 copy-start.1
  68.7 17.4 %all-to-all-start.6 = ((bf16[16,1,16,2048]{3,2,1,0:T(8,128)(2,1)}), bf16[16,1,16,2048]{3,2,1,0:T(8,128)(2,1)S(1)}, u32[]{:S(2)}, u32[]{:S(2)}) async-start(bf16[16,1,16,2048]{3,2,1,0:T(8,128)(2,1)} %stack.10), calls=%async_computation.10 | async-start | bytes 2097152 | tf_op jit(solution)/shard_map/all_to_all | solution.py:56
  72.4 170.6 %reduce-scatter.13.cloned.1.call-start = ((), (), s32[]{:S(2)}) async-start(), calls=%async_computation.22 | async-start | bytes 737280 | tf_op jit(solution)/shard_map/reduce_scatter | solution.py:68
  72.4 2.5 copy-start.7
  75.7 1.2 copy-start.4
  75.7 1.3 copy-start.5
  87.3 17.7 %all-to-all-start.9 = ((bf16[16,1,16,2048]{3,2,1,0:T(8,128)(2,1)}), bf16[16,1,16,2048]{3,2,1,0:T(8,128)(2,1)}, u32[]{:S(2)}, u32[]{:S(2)}) async-start(bf16[16,1,16,2048]{3,2,1,0:T(8,128)(2,1)} %stack.11), calls=%async_computation.15 | async-start | bytes 2097152 | tf_op jit(solution)/shard_map/all_to_all | solution.py:56
  91.6 276.5 %reduce-scatter.17.cloned.1.call-start = ((), (), s32[]{:S(2)}) async-start(), calls=%async_computation.24 | async-start | bytes 737280 | tf_op jit(solution)/shard_map/reduce_scatter | solution.py:68
  91.7 1.6 copy-start.8
  105.0 2.5 copy-start.9
  109.8 11.1 %all-to-all-start.1 = ((bf16[1,16,2,576]{3,2,0,1:T(2,128)(2,1)}), bf16[1,16,2,576]{3,2,0,1:T(2,128)(2,1)S(1)}, u32[]{:S(2)}, u32[]{:S(2)}) async-start(bf16[1,16,2,576]{3,2,0,1:T(2,128)(2,1)} %copy.239), calls=%async_computation.2 | async-start | bytes 81920 | tf_op jit(solution)/shard_map/all_to_all | solution.py:72
  113.3 379.9 %reduce-scatter.21.cloned.1.call-start = ((), (), s32[]{:S(2)}) async-start(), calls=%async_computation.26 | async-start | bytes 737280 | tf_op jit(solution)/shard_map/reduce_scatter | solution.py:68
  114.5 504.4 %reduce-scatter.11.cloned.1.call-start = ((), (), s32[]{:S(2)}) async-start(), calls=%async_computation.21 | async-start | bytes 2228224 | tf_op jit(solution)/shard_map/reduce_scatter | solution.py:153
  244.5 11.1 %all-to-all-start.4 = ((bf16[1,16,2,576]{3,2,0,1:T(2,128)(2,1)}), bf16[1,16,2,576]{3,2,0,1:T(2,128)(2,1)S(1)}, u32[]{:S(2)}, u32[]{:S(2)}) async-start(bf16[1,16,2,576]{3,2,0,1:T(2,128)(2,1)} %copy.252), calls=%async_computation.7 | async-start | bytes 81920 | tf_op jit(solution)/shard_map/all_to_all | solution.py:72
  248.0 371.8 %reduce-scatter.15.cloned.1.call-start = ((), (), s32[]{:S(2)}) async-start(), calls=%async_computation.23 | async-start | bytes 2228224 | tf_op jit(solution)/shard_map/reduce_scatter | solution.py:153
  369.6 11.1 %all-to-all-start.7 = ((bf16[1,16,2,576]{3,2,0,1:T(2,128)(2,1)}), bf16[1,16,2,576]{3,2,0,1:T(2,128)(2,1)S(1)}, u32[]{:S(2)}, u32[]{:S(2)}) async-start(bf16[1,16,2,576]{3,2,0,1:T(2,128)(2,1)} %copy.266), calls=%async_computation.12 | async-start | bytes 81920 | tf_op jit(solution)/shard_map/all_to_all | solution.py:72
  373.1 247.6 %reduce-scatter.19.cloned.1.call-start = ((), (), s32[]{:S(2)}) async-start(), calls=%async_computation.25 | async-start | bytes 2228224 | tf_op jit(solution)/shard_map/reduce_scatter | solution.py:153
  494.8 11.1 %all-to-all-start.10 = ((bf16[1,16,2,576]{3,2,0,1:T(2,128)(2,1)}), bf16[1,16,2,576]{3,2,0,1:T(2,128)(2,1)S(1)}, u32[]{:S(2)}, u32[]{:S(2)}) async-start(bf16[1,16,2,576]{3,2,0,1:T(2,128)(2,1)} %copy.280), calls=%async_computation.17 | async-start | bytes 81920 | tf_op jit(solution)/shard_map/all_to_all | solution.py:72
  498.3 193.1 %reduce-scatter.23.cloned.1.call-start = ((), (), s32[]{:S(2)}) async-start(), calls=%async_computation.27 | async-start | bytes 2228224 | tf_op jit(solution)/shard_map/reduce_scatter | solution.py:153
  506.0 6.4 copy-start.3
Sparse Core Ops, SparseCore 0:
  57.6 33.2 reduce-scatter.8
  93.3 31.1 reduce-scatter.12
  126.9 30.1 reduce-scatter.16
  159.3 30.3 reduce-scatter.20
  243.0 73.0 reduce-scatter.10
  368.2 73.0 reduce-scatter.14
  493.3 72.9 reduce-scatter.18
  618.4 73.0 reduce-scatter.22
